TPU v7x, 32 devices: a whole 2x2x4 slice. The times are simulated.
32 devices in a mesh: space: 8 (over y, x, core), dp: 4 (over z).
Axes of the slice: x: 2, y: 2, z: 4, core: 2. Of those that a mesh axis runs over, the one named last changes fastest.
Arguments:
- block_in: bfloat16 [4, 8, 56, 56, 128], P('dp', 'space'), may hold values from -6 to 6
- weights: bfloat16 [3, 3, 128, 128], replicated, may hold values from -0.1875 to 0.1875
- out_bias: float32 [128], replicated, may hold values from -3 to 3
- adjacency: int32 [8, 8, 2], P('space'), may hold values from 0 to 7, as said below
- cotangent: bfloat16 [4, 8, 56, 56, 128], P('dp', 'space'), may hold values from -6 to 6
Outputs:
- block_out: bfloat16 [4, 8, 56, 56, 128], P('dp', 'space')
- weight_grad: float32 [3, 3, 128, 128], replicated
- grad_in: bfloat16 [4, 8, 56, 56, 128], P('dp', 'space')
Inputs may be any that keep to these rules, and one draw needn't show every extreme that they name: adjacency[t, e] = (p, f) for e < 4 means that adjacency[p, f] = (t, e): edges are glued in pairs; entries 4 + k hold a tile and corner k' with adjacency[p, 4 + k'] = (t, k), corners glued in pairs. The corner pairing need not follow the edge pairing. Every edge and every corner of every tile appears exactly once as a partner. Column 1 lies in 0..3.
All inputs are finite; a program needn't handle non-finite values.
Results may differ from a plain program's by a relative error of at most 0.0031.
Values may be sent and summed in bfloat16 or wider, within the bound.
A program may use at most 64 MiB of HBM per device.

v0:
```python
import jax
import jax.numpy as jnp
from jax import lax
from jax.sharding import PartitionSpec as P


def tile_edges(field):
    top_rim = field[0, :, :]
    right_rim = field[:, -1, :]
    bottom_rim = jnp.flip(field[-1, :, :], 0)
    left_rim = jnp.flip(field[:, 0, :], 0)
    return jnp.stack([top_rim, right_rim, bottom_rim, left_rim], 0)


def tile_corners(field):
    return jnp.stack([field[0, 0, :], field[0, -1, :], field[-1, -1, :], field[-1, 0, :]], 0)


def assemble(field, near_edges, near_corners):
    top_row = jnp.concatenate([near_corners[0:1], jnp.flip(near_edges[0], 0), near_corners[1:2]], 0)
    bottom_row = jnp.concatenate([near_corners[3:4], near_edges[2], near_corners[2:3]], 0)
    middle = jnp.concatenate(
        [near_edges[3][:, None], field, jnp.flip(near_edges[1], 0)[:, None]], 1
    )
    return jnp.concatenate([top_row[None], middle, bottom_row[None]], 0)


def conv_forward(padded, weights):
    side = padded.shape[0] - 2
    width = padded.shape[2]
    running = jnp.zeros((side * side, weights.shape[3]), jnp.float32)
    for row_off in range(3):
        for col_off in range(3):
            window = padded[row_off : row_off + side, col_off : col_off + side].reshape(
                side * side, width
            )
            running = running + jnp.dot(
                window, weights[row_off, col_off], preferred_element_type=jnp.float32
            )
    return running.reshape(side, side, -1)


def conv_backward(padded, grad_out, weights):
    side = padded.shape[0] - 2
    width = padded.shape[2]
    grad_rows = grad_out.reshape(side * side, -1)
    grad_pad = jnp.zeros(padded.shape, jnp.float32)
    kernel_rows = []
    for row_off in range(3):
        kernel_cols = []
        for col_off in range(3):
            window = padded[row_off : row_off + side, col_off : col_off + side].reshape(
                side * side, width
            )
            kernel_cols.append(jnp.dot(window.T, grad_rows, preferred_element_type=jnp.float32))
            back = jnp.dot(
                grad_rows, weights[row_off, col_off].T, preferred_element_type=jnp.float32
            )
            grad_pad = grad_pad + jnp.pad(
                back.reshape(side, side, width),
                ((row_off, 2 - row_off), (col_off, 2 - col_off), (0, 0)),
            )
        kernel_rows.append(jnp.stack(kernel_cols, 0))
    return (jnp.stack(kernel_rows, 0), grad_pad)


def rim_grads(grad_pad):
    top_rim = grad_pad[0, 1:-1]
    right_rim = grad_pad[1:-1, -1]
    bottom_rim = jnp.flip(grad_pad[-1, 1:-1], 0)
    left_rim = jnp.flip(grad_pad[1:-1, 0], 0)
    rim_edges = jnp.stack([top_rim, right_rim, bottom_rim, left_rim], 0).astype(jnp.bfloat16)
    rim_corners = jnp.stack(
        [grad_pad[0, 0], grad_pad[0, -1], grad_pad[-1, -1], grad_pad[-1, 0]], 0
    ).astype(jnp.bfloat16)
    return (rim_edges, rim_corners)


def add_back(interior, back_edges, back_corners):
    edge_vals = back_edges.astype(jnp.float32)
    corner_vals = back_corners.astype(jnp.float32)
    interior = interior.at[0, :].add(jnp.flip(edge_vals[0], 0))
    interior = interior.at[:, -1].add(jnp.flip(edge_vals[1], 0))
    interior = interior.at[-1, :].add(edge_vals[2])
    interior = interior.at[:, 0].add(edge_vals[3])
    interior = interior.at[0, 0].add(corner_vals[0])
    interior = interior.at[0, -1].add(corner_vals[1])
    interior = interior.at[-1, -1].add(corner_vals[2])
    interior = interior.at[-1, 0].add(corner_vals[3])
    return interior


def glue(edge_cells, corner_cells, link_rows, backward):
    edge_tile = link_rows[0:4, 0]
    edge_side = link_rows[0:4, 1]
    corner_tile = link_rows[4:8, 0]
    corner_side = link_rows[4:8, 1]
    tile_count = lax.axis_size("space")
    tile_ids = jnp.arange(tile_count, dtype=jnp.int32)
    edge_hit = edge_tile[None, :] == tile_ids[:, None]
    corner_hit = corner_tile[None, :] == tile_ids[:, None]
    outgoing = jnp.where(
        edge_hit[:, :, None, None], edge_cells[None], jnp.zeros((), edge_cells.dtype)
    )
    outgoing_corners = jnp.where(
        corner_hit[:, :, None], corner_cells[None], jnp.zeros((), corner_cells.dtype)
    )
    if backward:
        arrived, arrived_corners = (
            lax.all_to_all(outgoing, "space", split_axis=0, concat_axis=0, tiled=True),
            lax.all_to_all(outgoing_corners, "space", split_axis=0, concat_axis=0, tiled=True),
        )
    else:
        arrived, arrived_corners = (
            lax.all_to_all(outgoing, "space", split_axis=0, concat_axis=0, tiled=True),
            lax.all_to_all(outgoing_corners, "space", split_axis=0, concat_axis=0, tiled=True),
        )
    return (arrived[edge_tile, edge_side], arrived_corners[corner_tile, corner_side])


def per_device(block_in, weights, out_bias, adjacency, cotangent):
    inputs = block_in[0, 0]
    link_rows = adjacency[0]
    activation = jax.nn.silu(inputs.astype(jnp.float32)).astype(jnp.bfloat16)
    near_edges, near_corners = glue(
        tile_edges(activation), tile_corners(activation), link_rows, False
    )
    padded = assemble(activation, near_edges, near_corners)
    conv_sum = conv_forward(padded, weights)
    result = (inputs.astype(jnp.float32) + conv_sum + out_bias).astype(jnp.bfloat16)
    grad_out = cotangent[0, 0]
    local_kernel, grad_pad = conv_backward(padded, grad_out, weights)
    rim_edges, rim_corners = rim_grads(grad_pad)
    back_edges, back_corners = glue(rim_edges, rim_corners, link_rows, True)
    act_grad = add_back(grad_pad[1:-1, 1:-1], back_edges, back_corners)
    input_f = inputs.astype(jnp.float32)
    sigmoid_x = jax.nn.sigmoid(input_f)
    grad_in = (
        grad_out.astype(jnp.float32) + act_grad * sigmoid_x * (1.0 + input_f * (1.0 - sigmoid_x))
    ).astype(jnp.bfloat16)
    weight_grad = lax.psum(local_kernel, ("space", "dp"))
    return (result[None, None], weight_grad, grad_in[None, None])


def solution(mesh):
    placed = (
        P("dp", "space", None, None, None),
        P(),
        P(),
        P("space", None, None),
        P("dp", "space", None, None, None),
    )
    return jax.shard_map(
        per_device,
        mesh=mesh,
        in_specs=placed,
        out_specs=(P("dp", "space", None, None, None), P(), P("dp", "space", None, None, None)),
        check_vma=False,
    )
```

profile of v0, /device:TPU:0, one launch (start us, length us, event | category | flops | bytes accessed | tf_op | source)
XLA Modules:
  0.0 241.1 jit_solution(15127318088615724658)
XLA Ops:
  7.2 1.8 fusion.20
  13.6 1.2 pad_add_fusion
  14.8 1.0 copy.103
  17.5 5.2 %all-to-all-start.3 = ((bf16[8,4,128]{2,1,0:T(4,128)(2,1)}), bf16[8,4,128]{2,1,0:T(4,128)(2,1)}, u32[]{:S(2)}, u32[]{:S(2)}) async-start(bf16[8,4,128]{2,1,0:T(4,128)(2,1)} %broadcast_select_fusion.2), calls=%async_computation.3 | async-start | bytes 16384 | tf_op jit(solution)/shard_map/all_to_all | solution.py:111
  22.6 0.9 slice.471
  28.3 0.9 broadcast_select_fusion
  29.2 4.2 %all-to-all-start.2 = ((bf16[8,4,56,128]{3,2,1,0:T(8,128)(2,1)}), bf16[8,4,56,128]{3,2,1,0:T(8,128)(2,1)}, u32[]{:S(2)}, u32[]{:S(2)}) async-start(bf16[8,4,56,128]{3,2,1,0:T(8,128)(2,1)} %broadcast_select_fusion), calls=%async_computation.2 | async-start | bytes 917504 | tf_op jit(solution)/shard_map/all_to_all | solution.py:110
  34.1 1.5 copy.102
  35.6 1.0 copy.45
  37.2 0.8 and_reduce_fusion
  38.0 1.3 gather_fusion.3
  39.3 3.2 %all-to-all-done.2 = bf16[8,4,56,128]{3,2,1,0:T(8,128)(2,1)} async-done(((bf16[8,4,56,128]{3,2,1,0:T(8,128)(2,1)}), bf16[8,4,56,128]{3,2,1,0:T(8,128)(2,1)}, u32[]{:S(2)}, u32[]{:S(2)}) %all-to-all-start.2) | async-done | bytes 458784 | tf_op jit(solution)/shard_map/all_to_all | solution.py:110
  42.5 2.2 gather_fusion.2
  44.7 0.8 convert_element_type.76
  45.6 1.4 slice.479
  47.6 1.4 rev.32
  48.9 1.4 slice_add_fusion.2
  50.3 1.7 scatter-add.26
  52.0 1.4 fusion.67
  53.4 1.0 slice_add_fusion
  54.4 1.8 scatter-add.30
  56.1 0.8 fusion.66
  57.5 1.3 scatter-add.34
  58.8 2.6 %broadcast_select_fusion.4 = f32[1,1,128]{2,0,1:T(1,128)S(1)} fusion(pred[]{:T(512)} %and_reduce_fusion, f32[56,56,128]{2,0,1:T(8,128)} %scatter-add.34, s32[]{:T(128)} %bitcast.94, s32[]{:T(128)} %bitcast.95, f32[4,128]{1,0:T(4,128)S(1)} %convert_element_type.77), kind=kLoop, calls=%fused_computation.136 | loop fusion | flops 256 | bytes 1545 | tf_op jit(solution)/shard_map/select.13
  61.3 2.5 %scatter-add.35 = f32[56,56,128]{2,0,1:T(8,128)} dynamic-update-slice(f32[56,56,128]{2,0,1:T(8,128)} %scatter-add.34, f32[1,1,128]{2,0,1:T(1,128)S(1)} %broadcast_select_fusion.4, s32[]{:T(128)} %bitcast.94, s32[]{:T(128)} %bitcast.95, s32[]{:T(128)} %constant.227.clone.1) | dynamic-update-slice | bytes 1028 | tf_op jit(solution)/shard_map/scatter-add | solution.py:87
  64.6 1.3 scatter-add.36
  66.5 1.3 scatter-add.39
  67.8 2.2 fusion.19
  70.9 3.3 %all-to-all-start = ((bf16[8,4,128]{2,1,0:T(4,128)(2,1)}), bf16[8,4,128]{2,1,0:T(4,128)(2,1)S(1)}, u32[]{:S(2)}, u32[]{:S(2)}) async-start(bf16[8,4,128]{2,1,0:T(4,128)(2,1)} %broadcast_select_fusion.3), calls=%async_computation | async-start | bytes 16384 | tf_op jit(solution)/shard_map/all_to_all | solution.py:116
  74.3 0.9 broadcast_select_fusion.1
  75.1 3.7 %all-to-all-done = bf16[8,4,128]{2,1,0:T(4,128)(2,1)S(1)} async-done(((bf16[8,4,128]{2,1,0:T(4,128)(2,1)}), bf16[8,4,128]{2,1,0:T(4,128)(2,1)S(1)}, u32[]{:S(2)}, u32[]{:S(2)}) %all-to-all-start) | async-done | bytes 8224 | tf_op jit(solution)/shard_map/all_to_all | solution.py:116
  78.9 4.1 %all-to-all-start.1 = ((bf16[8,4,56,128]{3,2,1,0:T(8,128)(2,1)}), bf16[8,4,56,128]{3,2,1,0:T(8,128)(2,1)}, u32[]{:S(2)}, u32[]{:S(2)}) async-start(bf16[8,4,56,128]{3,2,1,0:T(8,128)(2,1)} %broadcast_select_fusion.1), calls=%async_computation.1 | async-start | bytes 917504 | tf_op jit(solution)/shard_map/all_to_all | solution.py:115
  83.2 2.2 convolution_bitcast_fusion.4
  85.4 1.0 copy.74
  87.0 5.1 %all-to-all-done.1 = bf16[8,4,56,128]{3,2,1,0:T(8,128)(2,1)} async-done(((bf16[8,4,56,128]{3,2,1,0:T(8,128)(2,1)}), bf16[8,4,56,128]{3,2,1,0:T(8,128)(2,1)}, u32[]{:S(2)}, u32[]{:S(2)}) %all-to-all-start.1) | async-done | bytes 458784 | tf_op jit(solution)/shard_map/all_to_all | solution.py:115
  92.1 1.6 gather_fusion.1
  95.9 1.5 fusion.46
  99.9 0.9 copy-done.6
  104.6 0.9 pad_maximum_fusion.3
  105.8 1.8 convolution_add_fusion.7
  108.0 0.8 copy-done.7
  109.1 0.8 copy-done.13
  110.6 0.8 copy-done.11
  111.8 0.8 copy-done.9
  112.9 0.8 copy-done.3
  114.7 1.0 copy.73
  115.7 116.7 %all-reduce.11.cloned.1.call-done = f32[3,3,128,128]{3,2,1,0:T(8,128)} async-done(((f32[3,3,128,128]{3,2,1,0:T(8,128)}), f32[3,3,128,128]{3,2,1,0:T(8,128)}) %all-reduce.11.cloned.1.call-update) | async-done | bytes 589840 | tf_op jit(solution)/shard_map/psum | solution.py:141
  232.4 1.9 copy.114
  (132 shorter events, 28.2 us)
Async XLA Ops:
  7.2 1.8 copy-start.14
  7.2 1.8 copy-start
  14.8 1.1 copy-start.24
  15.8 1.0 copy-start.16
  15.8 17.6 %copy-start.1 = (bf16[1,1,56,56,128]{4,3,2,1,0:T(8,128)(2,1)S(1)}, bf16[1,1,56,56,128]{4,3,2,1,0:T(8,128)(2,1)}, u32[]{:S(2)}) copy-start(bf16[1,1,56,56,128]{4,3,2,1,0:T(8,128)(2,1)} %param.21) | copy-start | bytes 2408452
  16.8 6.8 %copy-start.22 = (pred[8,4]{1,0:T(8,128)(4,1)}, pred[8,4]{1,0:T(8,128)(4,1)S(1)}, u32[]{:S(2)}) copy-start(pred[8,4]{1,0:T(8,128)(4,1)S(1)} %iota_compare_fusion.1) | copy-start | bytes 100
  17.5 11.7 %all-to-all-start.3 = ((bf16[8,4,128]{2,1,0:T(4,128)(2,1)}), bf16[8,4,128]{2,1,0:T(4,128)(2,1)}, u32[]{:S(2)}, u32[]{:S(2)}) async-start(bf16[8,4,128]{2,1,0:T(4,128)(2,1)} %broadcast_select_fusion.2), calls=%async_computation.3 | async-start | bytes 16384 | tf_op jit(solution)/shard_map/all_to_all | solution.py:111
  27.6 6.5 %copy-start.20 = (pred[8,4]{1,0:T(8,128)(4,1)}, pred[8,4]{1,0:T(8,128)(4,1)S(1)}, u32[]{:S(2)}) copy-start(pred[8,4]{1,0:T(8,128)(4,1)S(1)} %iota_compare_fusion) | copy-start | bytes 100
  29.2 13.3 %all-to-all-start.2 = ((bf16[8,4,56,128]{3,2,1,0:T(8,128)(2,1)}), bf16[8,4,56,128]{3,2,1,0:T(8,128)(2,1)}, u32[]{:S(2)}, u32[]{:S(2)}) async-start(bf16[8,4,56,128]{3,2,1,0:T(8,128)(2,1)} %broadcast_select_fusion), calls=%async_computation.2 | async-start | bytes 917504 | tf_op jit(solution)/shard_map/all_to_all | solution.py:110
  33.8 1.7 copy-start.12
  35.6 1.7 copy-start.25
  35.6 2.4 %copy-start.19 = (s32[4]{0:T(128)S(1)}, s32[4]{0:T(128)}, u32[]{:S(2)}) copy-start(s32[4]{0:T(128)} %get-tuple-element.139) | copy-start | bytes 52
  45.6 1.4 copy-start.17
  67.8 2.4 copy-start.23
  67.8 6.5 %copy-start.21 = (pred[8,4]{1,0:T(8,128)(4,1)S(1)}, pred[8,4]{1,0:T(8,128)(4,1)}, u32[]{:S(2)}) copy-start(pred[8,4]{1,0:T(8,128)(4,1)} %copy-done.20) | copy-start | bytes 100
  70.9 8.0 %all-to-all-start = ((bf16[8,4,128]{2,1,0:T(4,128)(2,1)}), bf16[8,4,128]{2,1,0:T(4,128)(2,1)S(1)}, u32[]{:S(2)}, u32[]{:S(2)}) async-start(bf16[8,4,128]{2,1,0:T(4,128)(2,1)} %broadcast_select_fusion.3), calls=%async_computation | async-start | bytes 16384 | tf_op jit(solution)/shard_map/all_to_all | solution.py:116
  78.9 13.2 %all-to-all-start.1 = ((bf16[8,4,56,128]{3,2,1,0:T(8,128)(2,1)}), bf16[8,4,56,128]{3,2,1,0:T(8,128)(2,1)}, u32[]{:S(2)}, u32[]{:S(2)}) async-start(bf16[8,4,56,128]{3,2,1,0:T(8,128)(2,1)} %broadcast_select_fusion.1), calls=%async_computation.1 | async-start | bytes 917504 | tf_op jit(solution)/shard_map/all_to_all | solution.py:115
  83.0 149.4 %all-reduce.11.cloned.1.call-start = ((), (), s32[]{:S(2)}) async-start(), calls=%async_computation.4 | async-start | bytes 1179648 | tf_op jit(solution)/shard_map/psum | solution.py:141
  94.9 1.0 copy-start.15
  98.4 0.9 copy-start.4
  99.9 0.9 copy-start.6
  101.8 0.9 copy-start.2
  102.7 0.9 copy-start.8
  103.1 1.4 copy-start.18
  103.6 0.9 copy-start.10
  104.5 1.4 copy-start.5
  107.6 1.1 copy-start.7
  108.8 1.1 copy-start.13
  110.2 1.2 copy-start.11
  111.4 1.1 copy-start.9
  112.5 1.1 copy-start.3
  113.7 0.7 copy-start.26
Sparse Core Ops, SparseCore 0:
  105.6 126.7 all-reduce.10
where the time goes:
time: 243 us; the launch traced here: 241 us
  waiting for transfers between devices  129 us (53%)
  local copies, waits for them, and re-layouts  42 us (17%)
  other arithmetic  21.2 us (9%)
  matrix products  17.5 us (7%)
  starting transfers between devices  17 us (7%)
  between operations  14.7 us (6%)
    psum x1, waiting for transfers between devices, per_device(): weight_grad = lax.psum(local_kernel, ('space', 'dp'))  117 us
    unnamed x60, local copies, waits for them, and re-layouts  13.6 us
    all_to_all x2, starting transfers between devices, glue(): lax.all_to_all(outgoing_corners, 'space', split_axis=0, concat_axis=0, ti...  8.5 us
    all_to_all x2, starting transfers between devices, glue(): lax.all_to_all(outgoing, 'space', split_axis=0, concat_axis=0, tiled=True)  8.32 us
    all_to_all x2, waiting for transfers between devices, glue(): lax.all_to_all(outgoing, 'space', split_axis=0, concat_axis=0, tiled=True)  8.3 us
    dot_general x9, matrix products, conv_backward(): jnp.dot(grad_rows, weights[row_off, col_off].T, preferred_element_type=jn...  6.31 us
    dot_general x9, matrix products, conv_forward(): jnp.dot(window, weights[row_off, col_off], preferred_element_type=jnp.flo...  5.74 us
    dot_general x9, matrix products, conv_backward(): jnp.dot(window.T, grad_rows, preferred_element_type=jnp.float32)  5.49 us
  transfers between devices with their start and end apart: 5, of which 4 were waited for; matrix products, arithmetic and copies ran while one was open for 9% of the time, Pallas kernels for 0%

commit v1 on v0

v1 whole, which is shorter than its diff:
```python
import functools

import jax
import jax.numpy as jnp
from jax import lax
from jax.experimental import pallas as pl
from jax.experimental.pallas import tpu as pltpu
from jax.sharding import PartitionSpec as P

MESH = pl.DeviceIdType.MESH
ROWS = 8
F32 = jnp.float32
BF16 = jnp.bfloat16


def silu(v):
    return v / (1.0 + jnp.exp(-v))


def wide_of(side):
    return -(-(side + 4) // 16) * 16


def block_kernel(
    n_sp, n_dp, side,
    adj, x_in, w_in, bias, g_in,
    out, wg_out, gin_out,
    taps, gtaps, pad_grad, wt, acc, col_a, col_b, fwd, back, wg, parts, dps, full,
    fs, fr, bs, br, ss, sr, ds_, dr, gs, gr,
):
    wide = wide_of(side)
    chan = 128
    chunks = side // ROWS
    me = lax.axis_index("space")
    my_dp = lax.axis_index("dp")

    barrier = pltpu.get_barrier_semaphore()

    def greet_sp(k, c):
        pl.semaphore_signal(barrier, inc=1, device_id=(lax.rem(me + k, n_sp), my_dp), device_id_type=MESH)
        return c

    def greet_dp(k, c):
        pl.semaphore_signal(barrier, inc=1, device_id=(me, lax.rem(my_dp + k, n_dp)), device_id_type=MESH)
        return c

    lax.fori_loop(1, n_sp, greet_sp, 0)
    lax.fori_loop(1, n_dp, greet_dp, 0)

    def at_sp(k):
        peer = lax.rem(me + k, n_sp)
        return peer, (peer, my_dp)

    def at_dp(k):
        peer = lax.rem(my_dp + k, n_dp)
        return peer, (me, peer)

    def gather_copy(buf, mine, where, send, recv, k):
        peer, dev = where(k)
        start = pltpu.make_async_remote_copy(
            src_ref=buf.at[mine], dst_ref=buf.at[mine], send_sem=send.at[peer],
            recv_sem=recv.at[mine], device_id=dev, device_id_type=MESH)
        wait = pltpu.make_async_remote_copy(
            src_ref=buf.at[mine], dst_ref=buf.at[peer], send_sem=send.at[peer],
            recv_sem=recv.at[peer], device_id=dev, device_id_type=MESH)
        return start, wait

    def begin(buf, mine, n, where, send, recv):
        def go(k, c):
            gather_copy(buf, mine, where, send, recv, k)[0].start()
            return c
        lax.fori_loop(1, n, go, 0)

    def finish(buf, mine, n, where, send, recv):
        def go(k, c):
            gather_copy(buf, mine, where, send, recv, k)[1].wait()
            return c
        lax.fori_loop(1, n, go, 0)

    r64 = lax.broadcasted_iota(jnp.int32, (wide, chan), 0)
    ra = lax.broadcasted_iota(jnp.int32, (wide, wide), 0)
    rb = lax.broadcasted_iota(jnp.int32, (wide, wide), 1)
    mirror = jnp.where(ra + rb == side - 1, 1.0, 0.0).astype(BF16)

    def flip(v):
        return jnp.dot(mirror, v, preferred_element_type=F32)

    s8 = lax.broadcasted_iota(jnp.int32, (ROWS, 8, chan), 1)

    def column(block, at):
        return jnp.sum(jnp.where(s8 == at, block, 0.0), axis=1)

    tail = jnp.zeros((wide - side, chan), F32)

    def widen(v):
        return jnp.concatenate([v, tail], axis=0)

    for c in range(chunks):
        lo = c * ROWS
        left = x_in[lo:lo + ROWS, 0:8, :].astype(F32)
        right = x_in[lo:lo + ROWS, side - 8:side, :].astype(F32)
        col_a[lo:lo + ROWS, :] = silu(column(left, 0))
        col_b[lo:lo + ROWS, :] = silu(column(right, 7))
    col_a[side:wide, :] = tail
    col_b[side:wide, :] = tail
    fwd[me, 0] = widen(silu(x_in[0].astype(F32))).astype(BF16)
    fwd[me, 1] = col_b[...].astype(BF16)
    fwd[me, 2] = flip(widen(silu(x_in[side - 1].astype(F32))).astype(BF16)).astype(BF16)
    fwd[me, 3] = flip(col_a[...].astype(BF16)).astype(BF16)
    pl.semaphore_wait(barrier, n_sp + n_dp - 2)
    begin(fwd, me, n_sp, at_sp, fs, fr)

    for r in range(3):
        for c in range(3):
            block = w_in[2 - r, (2 - c) * chan:(3 - c) * chan, :].astype(F32)
            wt[r, c * chan:(c + 1) * chan, :] = block.T.astype(BF16)
    zero_row = jnp.zeros((wide, 3 * chan), BF16)
    for row in (0, 1, side + 2, side + 3):
        gtaps[row] = zero_row

    def spread_grad(c, carry):
        for k in range(ROWS):
            i = c * ROWS + k
            g = widen(g_in[i].astype(F32))
            gtaps[i + 2, :, 0:chan] = pltpu.roll(g, 2, 0).astype(BF16)
            gtaps[i + 2, :, chan:2 * chan] = pltpu.roll(g, 1, 0).astype(BF16)
            gtaps[i + 2, :, 2 * chan:] = g.astype(BF16)
        return carry

    lax.fori_loop(0, chunks, spread_grad, 0)

    def grad_rows(first, count):
        total = jnp.zeros((count * wide, chan), F32)
        for r in range(3):
            total += jnp.dot(
                gtaps[pl.ds(first + r, count)].reshape(count * wide, 3 * chan), wt[r],
                preferred_element_type=F32)
        pad_grad[pl.ds(first, count)] = total.reshape(count, wide, chan)

    def grad_chunk(c, carry):
        grad_rows(c * ROWS, ROWS)
        return carry

    lax.fori_loop(0, chunks, grad_chunk, 0)
    grad_rows(side, 2)

    for c in range(chunks):
        lo = c * ROWS
        col_a[lo:lo + ROWS, :] = column(pad_grad[lo + 1:lo + 1 + ROWS, 0:8, :], 0)
        col_b[lo:lo + ROWS, :] = column(pad_grad[lo + 1:lo + 1 + ROWS, side:side + 8, :], 1)
    first_row = pad_grad[0]
    last_row = pad_grad[side + 1]
    top = pltpu.roll(first_row, wide - 1, 0)
    bottom = pltpu.roll(last_row, wide - 1, 0)

    def pack(v, corner):
        return jnp.where(r64 < side, v, jnp.where(r64 == side, corner, 0.0)).astype(BF16)

    back[me, 0] = pack(top, first_row[0:1])
    back[me, 1] = pack(col_b[...], first_row[side + 1:side + 2])
    back[me, 2] = pack(flip(bottom.astype(BF16)), last_row[side + 1:side + 2])
    back[me, 3] = pack(flip(col_a[...].astype(BF16)), last_row[0:1])
    begin(back, me, n_sp, at_sp, bs, br)

    def put_taps(row, a):
        taps[row, :, 0:chan] = pltpu.roll(a, 1, 0).astype(BF16)
        taps[row, :, chan:2 * chan] = a.astype(BF16)
        taps[row, :, 2 * chan:] = pltpu.roll(a, wide - 1, 0).astype(BF16)

    def spread_act(c, carry):
        for k in range(ROWS):
            i = c * ROWS + k
            put_taps(i + 1, widen(silu(x_in[i].astype(F32))))
        return carry

    lax.fori_loop(0, chunks, spread_act, 0)
    finish(fwd, me, n_sp, at_sp, fs, fr)

    def near(buf, e):
        return buf[adj[0, e, 0], adj[0, e, 1]]

    def near_corner(buf, k, row):
        return buf[adj[0, 4 + k, 0], adj[0, 4 + k, 1]].astype(F32)[row:row + 1]

    corner = [near_corner(fwd, k, 0) for k in range(4)]

    def rim_row(v, behind, ahead):
        return jnp.where(r64 < side, v, jnp.where(r64 == side, behind, jnp.where(r64 == wide - 1, ahead, 0.0)))

    put_taps(0, rim_row(flip(near(fwd, 0)), corner[1], corner[0]))
    put_taps(side + 1, rim_row(near(fwd, 2).astype(F32), corner[2], corner[3]))
    col_a[...] = near(fwd, 3).astype(F32)
    col_b[...] = flip(near(fwd, 1))
    s16 = lax.broadcasted_iota(jnp.int32, (ROWS, 16, chan), 1)
    at_right = (side - 1) // 16 * 16
    for c in range(chunks):
        lo = c * ROWS
        v = taps[lo + 1:lo + 1 + ROWS, 0:16, 0:chan].astype(F32)
        v = jnp.where(s16 == 0, col_a[lo:lo + ROWS, :][:, None, :], v)
        taps[lo + 1:lo + 1 + ROWS, 0:16, 0:chan] = v.astype(BF16)
        v = taps[lo + 1:lo + 1 + ROWS, at_right:at_right + 16, 2 * chan:].astype(F32)
        v = jnp.where(s16 == side - 1 - at_right, col_b[lo:lo + ROWS, :][:, None, :], v)
        taps[lo + 1:lo + 1 + ROWS, at_right:at_right + 16, 2 * chan:] = v.astype(BF16)

    acc[...] = jnp.zeros_like(acc)

    def kernel_chunk(c, carry):
        i0 = c * ROWS
        gt = gtaps[pl.ds(i0 + 2, ROWS), :, 2 * chan:].reshape(ROWS * wide, chan).T
        for r in range(3):
            acc[r] += jnp.dot(
                gt, taps[pl.ds(i0 + r, ROWS)].reshape(ROWS * wide, 3 * chan),
                preferred_element_type=F32)
        return carry

    lax.fori_loop(0, chunks, kernel_chunk, 0)
    for r in range(3):
        for c in range(3):
            at = (3 * r + c) * chan
            wg[at:at + chan, :] = acc[r, :, c * chan:(c + 1) * chan].T.astype(BF16)
    size = parts.shape[1]
    used = 9 * chan
    if n_sp * size > used:
        wg[used:, :] = jnp.zeros((n_sp * size - used, chan), BF16)

    def scatter_copy(k):
        peer, dev = at_sp(k)
        src = wg.at[pl.ds(pl.multiple_of(peer * size, 16), size)]
        start = pltpu.make_async_remote_copy(
            src_ref=src, dst_ref=parts.at[me], send_sem=ss.at[peer],
            recv_sem=sr.at[me], device_id=dev, device_id_type=MESH)
        wait = pltpu.make_async_remote_copy(
            src_ref=src, dst_ref=parts.at[peer], send_sem=ss.at[peer],
            recv_sem=sr.at[peer], device_id=dev, device_id_type=MESH)
        return start, wait

    def scatter_start(k, c):
        scatter_copy(k)[0].start()
        return c

    def scatter_wait(k, c):
        scatter_copy(k)[1].wait()
        return c

    lax.fori_loop(1, n_sp, scatter_start, 0)
    parts[me] = wg[pl.ds(pl.multiple_of(me * size, 16), size), :]

    def conv_chunk(c, carry):
        i0 = c * ROWS
        total = jnp.zeros((ROWS * wide, chan), F32)
        for r in range(3):
            total += jnp.dot(
                taps[pl.ds(i0 + r, ROWS)].reshape(ROWS * wide, 3 * chan), w_in[r],
                preferred_element_type=F32)
        conv = total.reshape(ROWS, wide, chan)[:, :side, :]
        field = x_in[pl.ds(i0, ROWS)].astype(F32)
        out[pl.ds(i0, ROWS)] = (field + conv + bias[...].reshape(1, 1, chan)).astype(BF16)
        return carry

    lax.fori_loop(0, chunks, conv_chunk, 0)

    lax.fori_loop(1, n_sp, scatter_wait, 0)
    mine = lax.fori_loop(0, n_sp, lambda k, t: t + parts[k].astype(F32), jnp.zeros((size, chan), F32))
    dps[my_dp] = mine.astype(BF16)
    begin(dps, my_dp, n_dp, at_dp, ds_, dr)

    finish(back, me, n_sp, at_sp, bs, br)

    def inner(v):
        return jnp.where(r64 < side, v, 0.0)

    ends = [near_corner(back, k, side) for k in range(4)]
    pad_grad[1] += pltpu.roll(inner(flip(near(back, 0))), 1, 0)
    pad_grad[side] += pltpu.roll(inner(near(back, 2).astype(F32)), 1, 0)
    col_a[...] = inner(near(back, 3).astype(F32)) + jnp.where(r64 == 0, ends[0], jnp.where(r64 == side - 1, ends[3], 0.0))
    col_b[...] = inner(flip(near(back, 1))) + jnp.where(r64 == 0, ends[1], jnp.where(r64 == side - 1, ends[2], 0.0))

    r56 = lax.broadcasted_iota(jnp.int32, (side, chan), 0)

    def finish_rows(c, carry):
        for k in range(ROWS):
            i = c * ROWS + k
            p = pltpu.roll(pad_grad[i + 1], wide - 1, 0)[:side]
            p = p + jnp.where(r56 == 0, col_a[pl.ds(i, 1), :], jnp.where(r56 == side - 1, col_b[pl.ds(i, 1), :], 0.0))
            v = x_in[i].astype(F32)
            s = 1.0 / (1.0 + jnp.exp(-v))
            gin_out[i] = (g_in[i].astype(F32) + p * s * (1.0 + v * (1.0 - s))).astype(BF16)
        return carry

    lax.fori_loop(0, chunks, finish_rows, 0)

    finish(dps, my_dp, n_dp, at_dp, ds_, dr)
    total = dps[0].astype(F32)
    for d in range(1, n_dp):
        total = total + dps[d].astype(F32)
    full[me] = total.astype(BF16)
    begin(full, me, n_sp, at_sp, gs, gr)
    finish(full, me, n_sp, at_sp, gs, gr)
    if n_sp * size > used:
        wg_out[...] = full[...].astype(F32).reshape(n_sp * size, chan)[:used]
    else:
        wg_out[...] = full[...].astype(F32).reshape(n_sp * size, chan)


def per_device(n_sp, n_dp, block_in, weights, out_bias, adjacency, cotangent):
    side, chan = block_in.shape[2], block_in.shape[4]
    wide = wide_of(side)
    size = -(-9 * chan // (16 * n_sp)) * 16
    vmem = pl.BlockSpec(memory_space=pltpu.VMEM)
    sem = pltpu.SemaphoreType.DMA
    result, wgrad, grad_in = pl.pallas_call(
        functools.partial(block_kernel, n_sp, n_dp, side),
        out_shape=(
            jax.ShapeDtypeStruct((side, side, chan), BF16),
            jax.ShapeDtypeStruct((9 * chan, chan), F32),
            jax.ShapeDtypeStruct((side, side, chan), BF16),
        ),
        in_specs=[pl.BlockSpec(memory_space=pltpu.SMEM), vmem, vmem, vmem, vmem],
        out_specs=(vmem, vmem, vmem),
        scratch_shapes=[
            pltpu.VMEM((side + 2, wide, 3 * chan), BF16),
            pltpu.VMEM((side + 4, wide, 3 * chan), BF16),
            pltpu.VMEM((side + 2, wide, chan), F32),
            pltpu.VMEM((3, 3 * chan, chan), BF16),
            pltpu.VMEM((3, chan, 3 * chan), F32),
            pltpu.VMEM((wide, chan), F32),
            pltpu.VMEM((wide, chan), F32),
            pltpu.VMEM((n_sp, 4, wide, chan), BF16),
            pltpu.VMEM((n_sp, 4, wide, chan), BF16),
            pltpu.VMEM((n_sp * size, chan), BF16),
            pltpu.VMEM((n_sp, size, chan), BF16),
            pltpu.VMEM((n_dp, size, chan), BF16),
            pltpu.VMEM((n_sp, size, chan), BF16),
            sem((n_sp,)), sem((n_sp,)), sem((n_sp,)), sem((n_sp,)), sem((n_sp,)), sem((n_sp,)),
            sem((n_dp,)), sem((n_dp,)), sem((n_sp,)), sem((n_sp,)),
        ],
        compiler_params=pltpu.CompilerParams(
            collective_id=0, has_side_effects=True, vmem_limit_bytes=56 * 2**20),
    )(
        adjacency, block_in[0, 0], weights.reshape(3, 3 * chan, chan), out_bias.reshape(1, chan),
        cotangent[0, 0],
    )
    return (result[None, None], wgrad.reshape(weights.shape), grad_in[None, None])


def solution(mesh):
    placed = (
        P("dp", "space", None, None, None),
        P(),
        P(),
        P("space", None, None),
        P("dp", "space", None, None, None),
    )
    return jax.shard_map(
        functools.partial(per_device, mesh.shape["space"], mesh.shape["dp"]),
        mesh=mesh,
        in_specs=placed,
        out_specs=(P("dp", "space", None, None, None), P(), P("dp", "space", None, None, None)),
        check_vma=False,
    )
```

time: 243 us -> 40.7 us (0.17)
  waiting for transfers between devices: 129 us -> 0 us
  local copies, waits for them, and re-layouts: 42 us -> 5.73 us
  Pallas kernels: 0 us -> 34.1 us
  other arithmetic: 21.2 us -> 0 us
  matrix products: 17.5 us -> 0 us
  starting transfers between devices: 17 us -> 0 us
  between operations: 14.7 us -> 0.66 us
    psum x1 -> x0, waiting for transfers between devices: 117 us -> none  [per_device(): weight_grad = lax.psum(local_kernel, ('space', 'dp'))]
    pallas_call x0 -> x1, Pallas kernels: none -> 34.1 us  [per_device(): pl.pallas_call(functools.partial(block_kernel, n_sp, n_dp, side), out_sha...]
    dot_general x27 -> x0, matrix products: 17.5 us -> none  [the longest x9 6.31 us: conv_backward(): jnp.dot(grad_rows, weights[row_off, col_off].T, preferred_element_type=jn...]
    all_to_all x4 -> x0, starting transfers between devices: 16.8 us -> none  [the longest x2 8.5 us: glue(): lax.all_to_all(outgoing_corners, 'space', split_axis=0, concat_axis=0, ti...]
    all_to_all x4 -> x0, waiting for transfers between devices: 12 us -> none  [the longest x2 8.3 us: glue(): lax.all_to_all(outgoing, 'space', split_axis=0, concat_axis=0, tiled=True)]
    scatter-add x7 -> x0, local copies, waits for them, and re-layouts: 10.5 us -> none  [the longest x1 2.54 us: add_back(): interior = interior.at[0, -1].add(corner_vals[1])]
    unnamed x60 -> x10, local copies, waits for them, and re-layouts: 13.6 us -> 5.73 us
    add x7 -> x0, other arithmetic: 5.65 us -> none  [the longest x1 1.36 us: add_back(): interior = interior.at[0, :].add(jnp.flip(edge_vals[0], 0))]
  transfers between devices with their start and end apart: 5 -> 0, of which waited for: 4 -> 0; matrix products, arithmetic and copies ran while one was open for 9% -> 0% of each run, Pallas kernels for 0% -> 0%
where the time goes in v1:
time: 40.7 us; the launch traced here: 40.5 us
  Pallas kernels  34.1 us (84%)
  local copies, waits for them, and re-layouts  5.73 us (14%)
  between operations  0.66 us (2%)
    pallas_call x1, Pallas kernels, per_device(): pl.pallas_call(functools.partial(block_kernel, n_sp, n_dp, side), out_sha...  34.1 us
    unnamed x10, local copies, waits for them, and re-layouts  5.73 us

profile of v1, /device:TPU:0, one launch (start us, length us, event | category | flops | bytes accessed | tf_op | source)
XLA Modules:
  0.0 40.5 jit_solution(17092743650470663756)
XLA Ops:
  0.6 0.0 copy-start.2
  0.6 0.7 %copy-done.2 = s32[1,8,2]{1,2,0:T(2,128)S(1)} copy-done((s32[1,8,2]{1,2,0:T(2,128)S(1)}, s32[1,8,2]{1,2,0:T(2,128)}, u32[]{:S(2)}) %copy-start.2) | copy-done | bytes 88
  1.3 0.7 %copy.8.adj = s32[1,8,2]{2,1,0:T(8,128)} copy(s32[1,8,2]{1,2,0:T(2,128)S(1)} %copy-done.2) | data formatting | bytes 128 | tf_op args[3]
  2.0 34.1 %shard_map.76 = (bf16[56,56,128]{2,1,0:T(8,128)(2,1)}, f32[1152,128]{1,0:T(8,128)}, bf16[56,56,128]{2,1,0:T(8,128)(2,1)}) custom-call(s32[1,8,2]{2,1,0:T(8,128)} %copy.8.adj, bf16[56,56,128]{2,1,0:T(8,128)(2,1)} %bitcast.7, bf16[3,384,128]{2,1,0:T(8,128)(2,1)} %bitcast.12, f32[1,128]{1,0:T(1,128)} %bitcast.13, bf16[56,56,128]{2,1,0:T(8,128)(2,1)} %bitcast.8), custom_call_target="tpu_custom_call" | custom-call | tf_op jit(solution)/shard_map/pallas_call | solution.py:311
  36.1 0.0 copy-start.1
  36.1 2.1 %copy.12 = bf16[1,1,56,56,128]{4,3,2,1,0:T(8,128)(2,1)} copy(bf16[1,1,56,56,128]{4,3,2,1,0:T(8,128)(2,1)} %bitcast.10) | data formatting | bytes 1605632
  38.2 0.0 copy-done.1
  38.2 0.0 copy-start
  38.2 0.8 %copy.13 = f32[3,3,128,128]{3,2,1,0:T(8,128)} copy(f32[3,3,128,128]{3,2,1,0:T(8,128)S(1)} %bitcast.11) | data formatting | bytes 1179648
  39.0 0.5 %copy-done = bf16[56,56,128]{2,1,0:T(8,128)(2,1)S(1)} copy-done((bf16[56,56,128]{2,1,0:T(8,128)(2,1)S(1)}, bf16[56,56,128]{2,1,0:T(8,128)(2,1)}, u32[]{:S(2)}) %copy-start) | copy-done | bytes 802840
  39.6 0.9 %copy.14 = bf16[1,1,56,56,128]{4,3,2,1,0:T(8,128)(2,1)} copy(bf16[1,1,56,56,128]{4,3,2,1,0:T(8,128)(2,1)S(1)} %bitcast.9) | data formatting | bytes 1605632
Async XLA Ops:
  0.6 0.7 %copy-start.2 = (s32[1,8,2]{1,2,0:T(2,128)S(1)}, s32[1,8,2]{1,2,0:T(2,128)}, u32[]{:S(2)}) copy-start(s32[1,8,2]{1,2,0:T(2,128)} %param.8) | copy-start | bytes 196
  36.1 2.2 %copy-start.1 = (f32[1152,128]{1,0:T(8,128)S(1)}, f32[1152,128]{1,0:T(8,128)}, u32[]{:S(2)}) copy-start(f32[1152,128]{1,0:T(8,128)} %get-tuple-element.7) | copy-start | bytes 1769476
  38.2 1.4 %copy-start = (bf16[56,56,128]{2,1,0:T(8,128)(2,1)S(1)}, bf16[56,56,128]{2,1,0:T(8,128)(2,1)}, u32[]{:S(2)}) copy-start(bf16[56,56,128]{2,1,0:T(8,128)(2,1)} %get-tuple-element.8) | copy-start | bytes 2408452

commit v2 on v1

--- a/solution.py
+++ b/solution.py
@@ -17,6 +17,20 @@
     return v / (1.0 + jnp.exp(-v))
 
 
+def encode(v):
+    top = jnp.maximum(jnp.max(jnp.abs(v), axis=0, keepdims=True), 1e-30)
+    power = jnp.ceil(jnp.log2(top))
+    code = jnp.clip(jnp.round(v * jnp.exp2(15.0 - power)), -32767.0, 32767.0)
+    rows = jnp.concatenate([code, jnp.broadcast_to(power, (16, v.shape[1]))], axis=0)
+    return rows.astype(jnp.int32).astype(jnp.int16)
+
+
+def decode(rows):
+    v = rows.astype(jnp.int32).astype(F32)
+    size = v.shape[0] - 16
+    return v[:size] * jnp.exp2(v[size:size + 1] - 15.0)
+
+
 def wide_of(side):
     return -(-(side + 4) // 16) * 16
 
@@ -24,9 +38,9 @@
 def block_kernel(
     n_sp, n_dp, side,
     adj, x_in, w_in, bias, g_in,
-    out, wg_out, gin_out,
+    out_hbm, wg_out, gin_hbm,
     taps, gtaps, pad_grad, wt, acc, col_a, col_b, fwd, back, wg, parts, dps, full,
-    fs, fr, bs, br, ss, sr, ds_, dr, gs, gr,
+    fs, fr, bs, br, ss, sr, ds_, dr, gs, gr, out, gin_out, wgf, lo_sem,
 ):
     wide = wide_of(side)
     chan = 128
@@ -160,7 +174,6 @@
     back[me, 1] = pack(col_b[...], first_row[side + 1:side + 2])
     back[me, 2] = pack(flip(bottom.astype(BF16)), last_row[side + 1:side + 2])
     back[me, 3] = pack(flip(col_a[...].astype(BF16)), last_row[0:1])
-    begin(back, me, n_sp, at_sp, bs, br)
 
     def put_taps(row, a):
         taps[row, :, 0:chan] = pltpu.roll(a, 1, 0).astype(BF16)
@@ -177,10 +190,10 @@
     finish(fwd, me, n_sp, at_sp, fs, fr)
 
     def near(buf, e):
-        return buf[adj[0, e, 0], adj[0, e, 1]]
+        return buf[adj[0, 0, e], adj[0, 1, e]]
 
     def near_corner(buf, k, row):
-        return buf[adj[0, 4 + k, 0], adj[0, 4 + k, 1]].astype(F32)[row:row + 1]
+        return buf[adj[0, 0, 4 + k], adj[0, 1, 4 + k]].astype(F32)[row:row + 1]
 
     corner = [near_corner(fwd, k, 0) for k in range(4)]
 
@@ -217,15 +230,15 @@
     for r in range(3):
         for c in range(3):
             at = (3 * r + c) * chan
-            wg[at:at + chan, :] = acc[r, :, c * chan:(c + 1) * chan].T.astype(BF16)
-    size = parts.shape[1]
+            wgf[at:at + chan, :] = acc[r, :, c * chan:(c + 1) * chan].T
+    size = parts.shape[1] - 16
     used = 9 * chan
     if n_sp * size > used:
-        wg[used:, :] = jnp.zeros((n_sp * size - used, chan), BF16)
+        wgf[used:, :] = jnp.zeros((n_sp * size - used, chan), F32)
 
     def scatter_copy(k):
         peer, dev = at_sp(k)
-        src = wg.at[pl.ds(pl.multiple_of(peer * size, 16), size)]
+        src = wg.at[peer]
         start = pltpu.make_async_remote_copy(
             src_ref=src, dst_ref=parts.at[me], send_sem=ss.at[peer],
             recv_sem=sr.at[me], device_id=dev, device_id_type=MESH)
@@ -234,7 +247,12 @@
             recv_sem=sr.at[peer], device_id=dev, device_id_type=MESH)
         return start, wait
 
+    def own_rows(peer):
+        return wgf[pl.ds(pl.multiple_of(peer * size, 16), size), :]
+
     def scatter_start(k, c):
+        peer = lax.rem(me + k, n_sp)
+        wg[peer] = encode(own_rows(peer))
         scatter_copy(k)[0].start()
         return c
 
@@ -243,7 +261,8 @@
         return c
 
     lax.fori_loop(1, n_sp, scatter_start, 0)
-    parts[me] = wg[pl.ds(pl.multiple_of(me * size, 16), size), :]
+    parts[me] = encode(own_rows(me))
+    begin(back, me, n_sp, at_sp, bs, br)
 
     def conv_chunk(c, carry):
         i0 = c * ROWS
@@ -258,10 +277,12 @@
         return carry
 
     lax.fori_loop(0, chunks, conv_chunk, 0)
+    out_copy = pltpu.make_async_copy(out, out_hbm, lo_sem.at[0])
+    out_copy.start()
 
     lax.fori_loop(1, n_sp, scatter_wait, 0)
-    mine = lax.fori_loop(0, n_sp, lambda k, t: t + parts[k].astype(F32), jnp.zeros((size, chan), F32))
-    dps[my_dp] = mine.astype(BF16)
+    mine = lax.fori_loop(0, n_sp, lambda k, t: t + decode(parts[k]), jnp.zeros((size, chan), F32))
+    dps[my_dp] = encode(mine)
     begin(dps, my_dp, n_dp, at_dp, ds_, dr)
 
     finish(back, me, n_sp, at_sp, bs, br)
@@ -288,18 +309,36 @@
         return carry
 
     lax.fori_loop(0, chunks, finish_rows, 0)
+    gin_copy = pltpu.make_async_copy(gin_out, gin_hbm, lo_sem.at[1])
+    gin_copy.start()
 
     finish(dps, my_dp, n_dp, at_dp, ds_, dr)
-    total = dps[0].astype(F32)
+    total = decode(dps[0])
     for d in range(1, n_dp):
-        total = total + dps[d].astype(F32)
-    full[me] = total.astype(BF16)
+        total = total + decode(dps[d])
+    full[me] = encode(total)
     begin(full, me, n_sp, at_sp, gs, gr)
     finish(full, me, n_sp, at_sp, gs, gr)
-    if n_sp * size > used:
-        wg_out[...] = full[...].astype(F32).reshape(n_sp * size, chan)[:used]
-    else:
-        wg_out[...] = full[...].astype(F32).reshape(n_sp * size, chan)
+    def open_rows(k, c):
+        wgf[pl.ds(pl.multiple_of(k * size, 16), size), :] = decode(full[k])
+        return c
+
+    lax.fori_loop(0, n_sp, open_rows, 0)
+    kernel_copy = pltpu.make_async_copy(wgf.at[pl.ds(0, used)], wg_out, lo_sem.at[2])
+    kernel_copy.start()
+    kernel_copy.wait()
+    gin_copy.wait()
+    out_copy.wait()
+
+
+def hand_on(*refs):
+    count = len(refs) // 2
+    sems = refs[-1]
+    copies = [pltpu.make_async_copy(refs[k], refs[count + k], sems.at[k]) for k in range(count)]
+    for one in copies:
+        one.start()
+    for one in copies:
+        one.wait()
 
 
 def per_device(n_sp, n_dp, block_in, weights, out_bias, adjacency, cotangent):
@@ -307,16 +346,18 @@
     wide = wide_of(side)
     size = -(-9 * chan // (16 * n_sp)) * 16
     vmem = pl.BlockSpec(memory_space=pltpu.VMEM)
+    hbm = pl.BlockSpec(memory_space=pl.ANY)
     sem = pltpu.SemaphoreType.DMA
-    result, wgrad, grad_in = pl.pallas_call(
+    shapes = (
+        jax.ShapeDtypeStruct((side, side, chan), BF16),
+        jax.ShapeDtypeStruct((9 * chan, chan), F32),
+        jax.ShapeDtypeStruct((side, side, chan), BF16),
+    )
+    held = pl.pallas_call(
         functools.partial(block_kernel, n_sp, n_dp, side),
-        out_shape=(
-            jax.ShapeDtypeStruct((side, side, chan), BF16),
-            jax.ShapeDtypeStruct((9 * chan, chan), F32),
-            jax.ShapeDtypeStruct((side, side, chan), BF16),
-        ),
+        out_shape=shapes,
         in_specs=[pl.BlockSpec(memory_space=pltpu.SMEM), vmem, vmem, vmem, vmem],
-        out_specs=(vmem, vmem, vmem),
+        out_specs=(hbm, hbm, hbm),
         scratch_shapes=[
             pltpu.VMEM((side + 2, wide, 3 * chan), BF16),
             pltpu.VMEM((side + 4, wide, 3 * chan), BF16),
@@ -327,19 +368,30 @@
             pltpu.VMEM((wide, chan), F32),
             pltpu.VMEM((n_sp, 4, wide, chan), BF16),
             pltpu.VMEM((n_sp, 4, wide, chan), BF16),
-            pltpu.VMEM((n_sp * size, chan), BF16),
-            pltpu.VMEM((n_sp, size, chan), BF16),
-            pltpu.VMEM((n_dp, size, chan), BF16),
-            pltpu.VMEM((n_sp, size, chan), BF16),
+            pltpu.VMEM((n_sp, size + 16, chan), jnp.int16),
+            pltpu.VMEM((n_sp, size + 16, chan), jnp.int16),
+            pltpu.VMEM((n_dp, size + 16, chan), jnp.int16),
+            pltpu.VMEM((n_sp, size + 16, chan), jnp.int16),
             sem((n_sp,)), sem((n_sp,)), sem((n_sp,)), sem((n_sp,)), sem((n_sp,)), sem((n_sp,)),
             sem((n_dp,)), sem((n_dp,)), sem((n_sp,)), sem((n_sp,)),
+            pltpu.VMEM((side, side, chan), BF16),
+            pltpu.VMEM((side, side, chan), BF16),
+            pltpu.VMEM((n_sp * size, chan), F32),
+            sem((3,)),
         ],
         compiler_params=pltpu.CompilerParams(
             collective_id=0, has_side_effects=True, vmem_limit_bytes=56 * 2**20),
     )(
-        adjacency, block_in[0, 0], weights.reshape(3, 3 * chan, chan), out_bias.reshape(1, chan),
+        adjacency.transpose(0, 2, 1), block_in[0, 0], weights.reshape(3, 3 * chan, chan), out_bias.reshape(1, chan),
         cotangent[0, 0],
     )
+    result, wgrad, grad_in = pl.pallas_call(
+        hand_on,
+        out_shape=shapes,
+        in_specs=[hbm, hbm, hbm],
+        out_specs=(hbm, hbm, hbm),
+        scratch_shapes=[sem((3,))],
+    )(*held)
     return (result[None, None], wgrad.reshape(weights.shape), grad_in[None, None])
 
 

time: 40.7 us -> 105 us (2.58)
  Pallas kernels: 34.1 us -> 104 us
  local copies, waits for them, and re-layouts: 5.73 us -> 0 us
    pallas_call x0 -> x1, Pallas kernels: none -> 67.6 us  [per_device(): pl.pallas_call(hand_on, out_shape=shapes, in_specs=[hbm, hbm, hbm], out_s...]
    unnamed x10 -> x0, local copies, waits for them, and re-layouts: 5.73 us -> none
    pallas_call x1, Pallas kernels: 34.1 us -> 36.6 us  [per_device(): pl.pallas_call(functools.partial(block_kernel, n_sp, n_dp, side), out_sha...]
where the time goes in v2:
time: 105 us
  Pallas kernels  104 us (99%)
    pallas_call x1, Pallas kernels, per_device(): pl.pallas_call(hand_on, out_shape=shapes, in_specs=[hbm, hbm, hbm], out_s...  67.6 us
    pallas_call x1, Pallas kernels, per_device(): pl.pallas_call(functools.partial(block_kernel, n_sp, n_dp, side), out_sha...  36.6 us

profile of v2, /device:TPU:0, one launch (start us, length us, event | category | flops | bytes accessed | tf_op | source)
XLA Modules:
  0.0 104.9 jit_solution(9060981842563076231)
XLA Ops:
  0.6 36.6 %shard_map.76 = (bf16[56,56,128]{2,1,0:T(8,128)(2,1)}, f32[1152,128]{1,0:T(8,128)}, bf16[56,56,128]{2,1,0:T(8,128)(2,1)}) custom-call(s32[1,2,8]{2,1,0:T(2,128)} %bitcast.11, bf16[56,56,128]{2,1,0:T(8,128)(2,1)} %bitcast.8, bf16[3,384,128]{2,1,0:T(8,128)(2,1)} %bitcast.10, f32[1,128]{1,0:T(1,128)} %bitcast.12, bf16[56,56,128]{2,1,0:T(8,128)(2,1)} %bitcast.9), custom_call_target="tpu_custom_call" | custom-call | tf_op jit(solution)/shard_map/pallas_call | solution.py:356
  37.3 67.6 %shard_map.77 = (bf16[56,56,128]{2,1,0:T(8,128)(2,1)}, f32[1152,128]{1,0:T(8,128)}, bf16[56,56,128]{2,1,0:T(8,128)(2,1)}) custom-call(bf16[56,56,128]{2,1,0:T(8,128)(2,1)} %get-tuple-element.9.refs_0_, f32[1152,128]{1,0:T(8,128)} %get-tuple-element.10.refs_1_, bf16[56,56,128]{2,1,0:T(8,128)(2,1)} %get-tuple-element.11.refs_2_), custom_call_target="tpu_custom_call" | custom-call | tf_op jit(solution)/shard_map/pallas_call | solution.py:388

commit v3 on v2

--- a/solution.py
+++ b/solution.py
@@ -40,7 +40,7 @@
     adj, x_in, w_in, bias, g_in,
     out_hbm, wg_out, gin_hbm,
     taps, gtaps, pad_grad, wt, acc, col_a, col_b, fwd, back, wg, parts, dps, full,
-    fs, fr, bs, br, ss, sr, ds_, dr, gs, gr, out, gin_out, wgf, lo_sem,
+    fs, fr, bs, br, ss, sr, ds_, dr, gs, gr, out, gin_out, wgf, lo_sem, col_g,
 ):
     wide = wide_of(side)
     chan = 128
@@ -91,6 +91,43 @@
             return c
         lax.fori_loop(1, n, go, 0)
 
+    partner = me + 1 - 2 * lax.rem(me, 2)
+
+    def push(buf, slot, peer, send, recv):
+        return pltpu.make_async_remote_copy(
+            src_ref=buf.at[slot], dst_ref=buf.at[slot], send_sem=send,
+            recv_sem=recv.at[slot], device_id=(peer, my_dp), device_id_type=MESH)
+
+    def alike(k):
+        return lax.rem(me + 2 * k, n_sp)
+
+    def beside(tile):
+        return tile + 1 - 2 * lax.rem(tile, 2)
+
+    def pair_begin(buf, send, recv):
+        def go(k, c):
+            push(buf, me, alike(k), send.at[alike(k)], recv).start()
+            return c
+        lax.fori_loop(1, n_sp // 2, go, 0)
+        push(buf, me, partner, send.at[partner], recv).start()
+
+    def pair_relay(buf, send, recv):
+        def go(k, c):
+            tile = alike(k)
+            push(buf, tile, partner, send.at[beside(tile)], recv).wait_recv()
+            push(buf, tile, partner, send.at[beside(tile)], recv).start()
+            return c
+        lax.fori_loop(1, n_sp // 2, go, 0)
+
+    def pair_finish(buf, send, recv):
+        push(buf, partner, partner, send.at[partner], recv).wait()
+        def go(k, c):
+            tile = alike(k)
+            push(buf, me, tile, send.at[tile], recv).wait_send()
+            push(buf, beside(tile), partner, send.at[beside(tile)], recv).wait()
+            return c
+        lax.fori_loop(1, n_sp // 2, go, 0)
+
     r64 = lax.broadcasted_iota(jnp.int32, (wide, chan), 0)
     ra = lax.broadcasted_iota(jnp.int32, (wide, wide), 0)
     rb = lax.broadcasted_iota(jnp.int32, (wide, wide), 1)
@@ -115,15 +152,16 @@
         right = x_in[lo:lo + ROWS, side - 8:side, :].astype(F32)
         col_a[lo:lo + ROWS, :] = silu(column(left, 0))
         col_b[lo:lo + ROWS, :] = silu(column(right, 7))
+        col_g[0, lo:lo + ROWS, :] = column(g_in[lo:lo + ROWS, 0:8, :].astype(F32), 0)
+        col_g[1, lo:lo + ROWS, :] = column(g_in[lo:lo + ROWS, side - 8:side, :].astype(F32), 7)
     col_a[side:wide, :] = tail
     col_b[side:wide, :] = tail
+    col_g[0, side:wide, :] = tail
+    col_g[1, side:wide, :] = tail
     fwd[me, 0] = widen(silu(x_in[0].astype(F32))).astype(BF16)
     fwd[me, 1] = col_b[...].astype(BF16)
     fwd[me, 2] = flip(widen(silu(x_in[side - 1].astype(F32))).astype(BF16)).astype(BF16)
     fwd[me, 3] = flip(col_a[...].astype(BF16)).astype(BF16)
-    pl.semaphore_wait(barrier, n_sp + n_dp - 2)
-    begin(fwd, me, n_sp, at_sp, fs, fr)
-
     for r in range(3):
         for c in range(3):
             block = w_in[2 - r, (2 - c) * chan:(3 - c) * chan, :].astype(F32)
@@ -143,6 +181,36 @@
 
     lax.fori_loop(0, chunks, spread_grad, 0)
 
+    def put_taps(row, a):
+        taps[row, :, 0:chan] = pltpu.roll(a, 1, 0).astype(BF16)
+        taps[row, :, chan:2 * chan] = a.astype(BF16)
+        taps[row, :, 2 * chan:] = pltpu.roll(a, wide - 1, 0).astype(BF16)
+
+    def spread_act(c, carry):
+        for k in range(ROWS):
+            i = c * ROWS + k
+            put_taps(i + 1, widen(silu(x_in[i].astype(F32))))
+        return carry
+
+    lax.fori_loop(0, chunks, spread_act, 0)
+
+    taps[0] = zero_row
+    taps[side + 1] = zero_row
+    pl.semaphore_wait(barrier, n_sp + n_dp - 2)
+    pair_begin(fwd, fs, fr)
+
+    acc[...] = jnp.zeros_like(acc)
+
+    def kernel_chunk(c, carry):
+        i0 = c * ROWS
+        gt = gtaps[pl.ds(i0 + 2, ROWS), :, 2 * chan:].reshape(ROWS * wide, chan).T
+        for r in range(3):
+            acc[r] += jnp.dot(
+                gt, taps[pl.ds(i0 + r, ROWS)].reshape(ROWS * wide, 3 * chan),
+                preferred_element_type=F32)
+        return carry
+
+    lax.fori_loop(0, chunks, kernel_chunk, 0)
     def grad_rows(first, count):
         total = jnp.zeros((count * wide, chan), F32)
         for r in range(3):
@@ -157,6 +225,8 @@
 
     lax.fori_loop(0, chunks, grad_chunk, 0)
     grad_rows(side, 2)
+
+    pair_relay(fwd, fs, fr)
 
     for c in range(chunks):
         lo = c * ROWS
@@ -175,19 +245,7 @@
     back[me, 2] = pack(flip(bottom.astype(BF16)), last_row[side + 1:side + 2])
     back[me, 3] = pack(flip(col_a[...].astype(BF16)), last_row[0:1])
 
-    def put_taps(row, a):
-        taps[row, :, 0:chan] = pltpu.roll(a, 1, 0).astype(BF16)
-        taps[row, :, chan:2 * chan] = a.astype(BF16)
-        taps[row, :, 2 * chan:] = pltpu.roll(a, wide - 1, 0).astype(BF16)
-
-    def spread_act(c, carry):
-        for k in range(ROWS):
-            i = c * ROWS + k
-            put_taps(i + 1, widen(silu(x_in[i].astype(F32))))
-        return carry
-
-    lax.fori_loop(0, chunks, spread_act, 0)
-    finish(fwd, me, n_sp, at_sp, fs, fr)
+    pair_finish(fwd, fs, fr)
 
     def near(buf, e):
         return buf[adj[0, 0, e], adj[0, 1, e]]
@@ -204,6 +262,55 @@
     put_taps(side + 1, rim_row(near(fwd, 2).astype(F32), corner[2], corner[3]))
     col_a[...] = near(fwd, 3).astype(F32)
     col_b[...] = flip(near(fwd, 1))
+
+    def turned(v):
+        return v.astype(BF16).T
+
+    acc[0] += jnp.dot(turned(gtaps[2, :, 2 * chan:]), taps[0], preferred_element_type=F32)
+    acc[2] += jnp.dot(turned(gtaps[side + 1, :, 2 * chan:]), taps[side + 1], preferred_element_type=F32)
+    for e, rim in ((0, col_a), (1, col_b)):
+        gt = turned(col_g[e])
+        at = 2 * e * chan
+        for r, turn in ((0, 1), (1, 0), (2, wide - 1)):
+            v = pltpu.roll(rim[...], turn, 0) if turn else rim[...]
+            acc[r, :, at:at + chan] += jnp.dot(gt, v.astype(BF16), preferred_element_type=F32)
+    for r in range(3):
+        for c in range(3):
+            at = (3 * r + c) * chan
+            wgf[at:at + chan, :] = acc[r, :, c * chan:(c + 1) * chan].T
+    size = parts.shape[1] - 16
+    used = 9 * chan
+    if n_sp * size > used:
+        wgf[used:, :] = jnp.zeros((n_sp * size - used, chan), F32)
+
+    def scatter_copy(k):
+        peer, dev = at_sp(k)
+        src = wg.at[peer]
+        start = pltpu.make_async_remote_copy(
+            src_ref=src, dst_ref=parts.at[me], send_sem=ss.at[peer],
+            recv_sem=sr.at[me], device_id=dev, device_id_type=MESH)
+        wait = pltpu.make_async_remote_copy(
+            src_ref=src, dst_ref=parts.at[peer], send_sem=ss.at[peer],
+            recv_sem=sr.at[peer], device_id=dev, device_id_type=MESH)
+        return start, wait
+
+    def own_rows(peer):
+        return wgf[pl.ds(pl.multiple_of(peer * size, 16), size), :]
+
+    def scatter_start(k, c):
+        peer = lax.rem(me + k, n_sp)
+        wg[peer] = encode(own_rows(peer))
+        scatter_copy(k)[0].start()
+        return c
+
+    def scatter_wait(k, c):
+        scatter_copy(k)[1].wait()
+        return c
+
+    lax.fori_loop(1, n_sp, scatter_start, 0)
+    parts[me] = encode(own_rows(me))
+    pair_begin(back, bs, br)
+
     s16 = lax.broadcasted_iota(jnp.int32, (ROWS, 16, chan), 1)
     at_right = (side - 1) // 16 * 16
     for c in range(chunks):
@@ -215,54 +322,6 @@
         v = jnp.where(s16 == side - 1 - at_right, col_b[lo:lo + ROWS, :][:, None, :], v)
         taps[lo + 1:lo + 1 + ROWS, at_right:at_right + 16, 2 * chan:] = v.astype(BF16)
 
-    acc[...] = jnp.zeros_like(acc)
-
-    def kernel_chunk(c, carry):
-        i0 = c * ROWS
-        gt = gtaps[pl.ds(i0 + 2, ROWS), :, 2 * chan:].reshape(ROWS * wide, chan).T
-        for r in range(3):
-            acc[r] += jnp.dot(
-                gt, taps[pl.ds(i0 + r, ROWS)].reshape(ROWS * wide, 3 * chan),
-                preferred_element_type=F32)
-        return carry
-
-    lax.fori_loop(0, chunks, kernel_chunk, 0)
-    for r in range(3):
-        for c in range(3):
-            at = (3 * r + c) * chan
-            wgf[at:at + chan, :] = acc[r, :, c * chan:(c + 1) * chan].T
-    size = parts.shape[1] - 16
-    used = 9 * chan
-    if n_sp * size > used:
-        wgf[used:, :] = jnp.zeros((n_sp * size - used, chan), F32)
-
-    def scatter_copy(k):
-        peer, dev = at_sp(k)
-        src = wg.at[peer]
-        start = pltpu.make_async_remote_copy(
-            src_ref=src, dst_ref=parts.at[me], send_sem=ss.at[peer],
-            recv_sem=sr.at[me], device_id=dev, device_id_type=MESH)
-        wait = pltpu.make_async_remote_copy(
-            src_ref=src, dst_ref=parts.at[peer], send_sem=ss.at[peer],
-            recv_sem=sr.at[peer], device_id=dev, device_id_type=MESH)
-        return start, wait
-
-    def own_rows(peer):
-        return wgf[pl.ds(pl.multiple_of(peer * size, 16), size), :]
-
-    def scatter_start(k, c):
-        peer = lax.rem(me + k, n_sp)
-        wg[peer] = encode(own_rows(peer))
-        scatter_copy(k)[0].start()
-        return c
-
-    def scatter_wait(k, c):
-        scatter_copy(k)[1].wait()
-        return c
-
-    lax.fori_loop(1, n_sp, scatter_start, 0)
-    parts[me] = encode(own_rows(me))
-    begin(back, me, n_sp, at_sp, bs, br)
 
     def conv_chunk(c, carry):
         i0 = c * ROWS
@@ -284,8 +343,16 @@
     mine = lax.fori_loop(0, n_sp, lambda k, t: t + decode(parts[k]), jnp.zeros((size, chan), F32))
     dps[my_dp] = encode(mine)
     begin(dps, my_dp, n_dp, at_dp, ds_, dr)
-
-    finish(back, me, n_sp, at_sp, bs, br)
+    pair_relay(back, bs, br)
+
+    finish(dps, my_dp, n_dp, at_dp, ds_, dr)
+    total = decode(dps[0])
+    for d in range(1, n_dp):
+        total = total + decode(dps[d])
+    full[me] = encode(total)
+    begin(full, me, n_sp, at_sp, gs, gr)
+
+    pair_finish(back, bs, br)
 
     def inner(v):
         return jnp.where(r64 < side, v, 0.0)
@@ -312,12 +379,6 @@
     gin_copy = pltpu.make_async_copy(gin_out, gin_hbm, lo_sem.at[1])
     gin_copy.start()
 
-    finish(dps, my_dp, n_dp, at_dp, ds_, dr)
-    total = decode(dps[0])
-    for d in range(1, n_dp):
-        total = total + decode(dps[d])
-    full[me] = encode(total)
-    begin(full, me, n_sp, at_sp, gs, gr)
     finish(full, me, n_sp, at_sp, gs, gr)
     def open_rows(k, c):
         wgf[pl.ds(pl.multiple_of(k * size, 16), size), :] = decode(full[k])
@@ -331,13 +392,15 @@
     out_copy.wait()
 
 
-def hand_on(*refs):
-    count = len(refs) // 2
-    sems = refs[-1]
-    copies = [pltpu.make_async_copy(refs[k], refs[count + k], sems.at[k]) for k in range(count)]
-    for one in copies:
+def hand_on(a_in, b_in, c_in, a_out, b_out, c_out, a, b, c, sems):
+    loads = [pltpu.make_async_copy(src, mid, sems.at[k]) for k, (src, mid) in enumerate(((a_in, a), (b_in, b), (c_in, c)))]
+    stores = [pltpu.make_async_copy(mid, dst, sems.at[3 + k]) for k, (mid, dst) in enumerate(((a, a_out), (b, b_out), (c, c_out)))]
+    for one in loads:
         one.start()
-    for one in copies:
+    for load, store in zip(loads, stores):
+        load.wait()
+        store.start()
+    for one in stores:
         one.wait()
 
 
@@ -378,6 +441,7 @@
             pltpu.VMEM((side, side, chan), BF16),
             pltpu.VMEM((n_sp * size, chan), F32),
             sem((3,)),
+            pltpu.VMEM((2, wide, chan), F32),
         ],
         compiler_params=pltpu.CompilerParams(
             collective_id=0, has_side_effects=True, vmem_limit_bytes=56 * 2**20),
@@ -390,7 +454,7 @@
         out_shape=shapes,
         in_specs=[hbm, hbm, hbm],
         out_specs=(hbm, hbm, hbm),
-        scratch_shapes=[sem((3,))],
+        scratch_shapes=[pltpu.VMEM(one.shape, one.dtype) for one in shapes] + [sem((6,))],
     )(*held)
     return (result[None, None], wgrad.reshape(weights.shape), grad_in[None, None])
 

time: 105 us -> 35.9 us (0.34)
  Pallas kernels: 104 us -> 35 us
    pallas_call x1, Pallas kernels: 67.6 us -> 2.53 us  [per_device(): pl.pallas_call(hand_on, out_shape=shapes, in_specs=[hbm, hbm, hbm], out_s...]
    pallas_call x1, Pallas kernels: 36.6 us -> 32.5 us  [per_device(): pl.pallas_call(functools.partial(block_kernel, n_sp, n_dp, side), out_sha...]
where the time goes in v3:
time: 35.9 us; the launch traced here: 35.6 us
  Pallas kernels  35 us (97%)
  between operations  0.64 us (2%)
    pallas_call x1, Pallas kernels, per_device(): pl.pallas_call(functools.partial(block_kernel, n_sp, n_dp, side), out_sha...  32.5 us
    pallas_call x1, Pallas kernels, per_device(): pl.pallas_call(hand_on, out_shape=shapes, in_specs=[hbm, hbm, hbm], out_s...  2.53 us

profile of v3, /device:TPU:0, one launch (start us, length us, event | category | flops | bytes accessed | tf_op | source)
XLA Modules:
  0.0 35.6 jit_solution(13872097077545127056)
XLA Ops:
  0.6 32.5 %shard_map.76 = (bf16[56,56,128]{2,1,0:T(8,128)(2,1)}, f32[1152,128]{1,0:T(8,128)}, bf16[56,56,128]{2,1,0:T(8,128)(2,1)}) custom-call(s32[1,2,8]{2,1,0:T(2,128)} %bitcast.11, bf16[56,56,128]{2,1,0:T(8,128)(2,1)} %bitcast.8, bf16[3,384,128]{2,1,0:T(8,128)(2,1)} %bitcast.10, f32[1,128]{1,0:T(1,128)} %bitcast.12, bf16[56,56,128]{2,1,0:T(8,128)(2,1)} %bitcast.9), custom_call_target="tpu_custom_call" | custom-call | tf_op jit(solution)/shard_map/pallas_call | solution.py:419
  33.1 2.5 %shard_map.77 = (bf16[56,56,128]{2,1,0:T(8,128)(2,1)}, f32[1152,128]{1,0:T(8,128)}, bf16[56,56,128]{2,1,0:T(8,128)(2,1)}) custom-call(bf16[56,56,128]{2,1,0:T(8,128)(2,1)} %get-tuple-element.9.a_in, f32[1152,128]{1,0:T(8,128)} %get-tuple-element.10.b_in, bf16[56,56,128]{2,1,0:T(8,128)(2,1)} %get-tuple-element.11.c_in), custom_call_target="tpu_custom_call" | custom-call | tf_op jit(solution)/shard_map/pallas_call | solution.py:452

commit v4 on v3

--- a/solution.py
+++ b/solution.py
@@ -211,40 +211,7 @@
         return carry
 
     lax.fori_loop(0, chunks, kernel_chunk, 0)
-    def grad_rows(first, count):
-        total = jnp.zeros((count * wide, chan), F32)
-        for r in range(3):
-            total += jnp.dot(
-                gtaps[pl.ds(first + r, count)].reshape(count * wide, 3 * chan), wt[r],
-                preferred_element_type=F32)
-        pad_grad[pl.ds(first, count)] = total.reshape(count, wide, chan)
-
-    def grad_chunk(c, carry):
-        grad_rows(c * ROWS, ROWS)
-        return carry
-
-    lax.fori_loop(0, chunks, grad_chunk, 0)
-    grad_rows(side, 2)
-
     pair_relay(fwd, fs, fr)
-
-    for c in range(chunks):
-        lo = c * ROWS
-        col_a[lo:lo + ROWS, :] = column(pad_grad[lo + 1:lo + 1 + ROWS, 0:8, :], 0)
-        col_b[lo:lo + ROWS, :] = column(pad_grad[lo + 1:lo + 1 + ROWS, side:side + 8, :], 1)
-    first_row = pad_grad[0]
-    last_row = pad_grad[side + 1]
-    top = pltpu.roll(first_row, wide - 1, 0)
-    bottom = pltpu.roll(last_row, wide - 1, 0)
-
-    def pack(v, corner):
-        return jnp.where(r64 < side, v, jnp.where(r64 == side, corner, 0.0)).astype(BF16)
-
-    back[me, 0] = pack(top, first_row[0:1])
-    back[me, 1] = pack(col_b[...], first_row[side + 1:side + 2])
-    back[me, 2] = pack(flip(bottom.astype(BF16)), last_row[side + 1:side + 2])
-    back[me, 3] = pack(flip(col_a[...].astype(BF16)), last_row[0:1])
-
     pair_finish(fwd, fs, fr)
 
     def near(buf, e):
@@ -309,7 +276,6 @@
 
     lax.fori_loop(1, n_sp, scatter_start, 0)
     parts[me] = encode(own_rows(me))
-    pair_begin(back, bs, br)
 
     s16 = lax.broadcasted_iota(jnp.int32, (ROWS, 16, chan), 1)
     at_right = (side - 1) // 16 * 16
@@ -323,6 +289,45 @@
         taps[lo + 1:lo + 1 + ROWS, at_right:at_right + 16, 2 * chan:] = v.astype(BF16)
 
 
+    def grad_rows(first, count):
+        total = jnp.zeros((count * wide, chan), F32)
+        for r in range(3):
+            total += jnp.dot(
+                gtaps[pl.ds(first + r, count)].reshape(count * wide, 3 * chan), wt[r],
+                preferred_element_type=F32)
+        pad_grad[pl.ds(first, count)] = total.reshape(count, wide, chan)
+
+    def grad_chunk(c, carry):
+        grad_rows(c * ROWS, ROWS)
+        return carry
+
+    lax.fori_loop(0, chunks, grad_chunk, 0)
+    grad_rows(side, 2)
+
+    for c in range(chunks):
+        lo = c * ROWS
+        col_a[lo:lo + ROWS, :] = column(pad_grad[lo + 1:lo + 1 + ROWS, 0:8, :], 0)
+        col_b[lo:lo + ROWS, :] = column(pad_grad[lo + 1:lo + 1 + ROWS, side:side + 8, :], 1)
+    first_row = pad_grad[0]
+    last_row = pad_grad[side + 1]
+    top = pltpu.roll(first_row, wide - 1, 0)
+    bottom = pltpu.roll(last_row, wide - 1, 0)
+
+    def pack(v, corner):
+        return jnp.where(r64 < side, v, jnp.where(r64 == side, corner, 0.0)).astype(BF16)
+
+    back[me, 0] = pack(top, first_row[0:1])
+    back[me, 1] = pack(col_b[...], first_row[side + 1:side + 2])
+    back[me, 2] = pack(flip(bottom.astype(BF16)), last_row[side + 1:side + 2])
+    back[me, 3] = pack(flip(col_a[...].astype(BF16)), last_row[0:1])
+
+    pair_begin(back, bs, br)
+
+    lax.fori_loop(1, n_sp, scatter_wait, 0)
+    mine = lax.fori_loop(0, n_sp, lambda k, t: t + decode(parts[k]), jnp.zeros((size, chan), F32))
+    dps[my_dp] = encode(mine)
+    begin(dps, my_dp, n_dp, at_dp, ds_, dr)
+
     def conv_chunk(c, carry):
         i0 = c * ROWS
         total = jnp.zeros((ROWS * wide, chan), F32)
@@ -339,10 +344,6 @@
     out_copy = pltpu.make_async_copy(out, out_hbm, lo_sem.at[0])
     out_copy.start()
 
-    lax.fori_loop(1, n_sp, scatter_wait, 0)
-    mine = lax.fori_loop(0, n_sp, lambda k, t: t + decode(parts[k]), jnp.zeros((size, chan), F32))
-    dps[my_dp] = encode(mine)
-    begin(dps, my_dp, n_dp, at_dp, ds_, dr)
     pair_relay(back, bs, br)
 
     finish(dps, my_dp, n_dp, at_dp, ds_, dr)

time: 35.9 us -> 33.6 us (0.936)
  Pallas kernels: 35 us -> 32.7 us
    pallas_call x1, Pallas kernels: 32.5 us -> 30.2 us  [per_device(): pl.pallas_call(functools.partial(block_kernel, n_sp, n_dp, side), out_sha...]
where the time goes in v4:
time: 33.6 us; the launch traced here: 33.4 us
  Pallas kernels  32.7 us (97%)
  between operations  0.64 us (2%)
    pallas_call x1, Pallas kernels, per_device(): pl.pallas_call(functools.partial(block_kernel, n_sp, n_dp, side), out_sha...  30.2 us
    pallas_call x1, Pallas kernels, per_device(): pl.pallas_call(hand_on, out_shape=shapes, in_specs=[hbm, hbm, hbm], out_s...  2.53 us

profile of v4, /device:TPU:0, one launch (start us, length us, event | category | flops | bytes accessed | tf_op | source)
XLA Modules:
  0.0 33.4 jit_solution(13337317738256711183)
XLA Ops:
  0.6 30.2 %shard_map.76 = (bf16[56,56,128]{2,1,0:T(8,128)(2,1)}, f32[1152,128]{1,0:T(8,128)}, bf16[56,56,128]{2,1,0:T(8,128)(2,1)}) custom-call(s32[1,2,8]{2,1,0:T(2,128)} %bitcast.11, bf16[56,56,128]{2,1,0:T(8,128)(2,1)} %bitcast.8, bf16[3,384,128]{2,1,0:T(8,128)(2,1)} %bitcast.10, f32[1,128]{1,0:T(1,128)} %bitcast.12, bf16[56,56,128]{2,1,0:T(8,128)(2,1)} %bitcast.9), custom_call_target="tpu_custom_call" | custom-call | tf_op jit(solution)/shard_map/pallas_call | solution.py:420
  30.8 2.5 %shard_map.77 = (bf16[56,56,128]{2,1,0:T(8,128)(2,1)}, f32[1152,128]{1,0:T(8,128)}, bf16[56,56,128]{2,1,0:T(8,128)(2,1)}) custom-call(bf16[56,56,128]{2,1,0:T(8,128)(2,1)} %get-tuple-element.9.a_in, f32[1152,128]{1,0:T(8,128)} %get-tuple-element.10.b_in, bf16[56,56,128]{2,1,0:T(8,128)(2,1)} %get-tuple-element.11.c_in), custom_call_target="tpu_custom_call" | custom-call | tf_op jit(solution)/shard_map/pallas_call | solution.py:453

commit v5 on v4

--- a/solution.py
+++ b/solution.py
@@ -381,28 +381,38 @@
     gin_copy.start()
 
     finish(full, me, n_sp, at_sp, gs, gr)
-    def open_rows(k, c):
-        wgf[pl.ds(pl.multiple_of(k * size, 16), size), :] = decode(full[k])
-        return c
-
-    lax.fori_loop(0, n_sp, open_rows, 0)
-    kernel_copy = pltpu.make_async_copy(wgf.at[pl.ds(0, used)], wg_out, lo_sem.at[2])
+    kernel_copy = pltpu.make_async_copy(full, wg_out, lo_sem.at[2])
     kernel_copy.start()
     kernel_copy.wait()
     gin_copy.wait()
     out_copy.wait()
 
 
-def hand_on(a_in, b_in, c_in, a_out, b_out, c_out, a, b, c, sems):
-    loads = [pltpu.make_async_copy(src, mid, sems.at[k]) for k, (src, mid) in enumerate(((a_in, a), (b_in, b), (c_in, c)))]
-    stores = [pltpu.make_async_copy(mid, dst, sems.at[3 + k]) for k, (mid, dst) in enumerate(((a, a_out), (b, b_out), (c, c_out)))]
+def hand_on(a_in, codes_in, c_in, a_out, wg_out, c_out, a, codes, c, wgf, sems):
+    first = pltpu.make_async_copy(codes_in, codes, sems.at[0])
+    loads = [pltpu.make_async_copy(a_in, a, sems.at[1]), pltpu.make_async_copy(c_in, c, sems.at[2])]
+    stores = [pltpu.make_async_copy(a, a_out, sems.at[3]), pltpu.make_async_copy(c, c_out, sems.at[4])]
+    used = wg_out.shape[0]
+    n_sp, rows = codes.shape[0], codes.shape[1]
+    size = rows - 16
+    last = pltpu.make_async_copy(wgf.at[pl.ds(0, used)], wg_out, sems.at[5])
+    first.start()
     for one in loads:
         one.start()
+    first.wait()
+
+    def open_rows(k, carry):
+        wgf[pl.ds(pl.multiple_of(k * size, 16), size), :] = decode(codes[k])
+        return carry
+
+    lax.fori_loop(0, n_sp, open_rows, 0)
+    last.start()
     for load, store in zip(loads, stores):
         load.wait()
         store.start()
     for one in stores:
         one.wait()
+    last.wait()
 
 
 def per_device(n_sp, n_dp, block_in, weights, out_bias, adjacency, cotangent):
@@ -417,9 +427,10 @@
         jax.ShapeDtypeStruct((9 * chan, chan), F32),
         jax.ShapeDtypeStruct((side, side, chan), BF16),
     )
+    codes = jax.ShapeDtypeStruct((n_sp, size + 16, chan), jnp.int16)
     held = pl.pallas_call(
         functools.partial(block_kernel, n_sp, n_dp, side),
-        out_shape=shapes,
+        out_shape=(shapes[0], codes, shapes[2]),
         in_specs=[pl.BlockSpec(memory_space=pltpu.SMEM), vmem, vmem, vmem, vmem],
         out_specs=(hbm, hbm, hbm),
         scratch_shapes=[
@@ -455,7 +466,7 @@
         out_shape=shapes,
         in_specs=[hbm, hbm, hbm],
         out_specs=(hbm, hbm, hbm),
-        scratch_shapes=[pltpu.VMEM(one.shape, one.dtype) for one in shapes] + [sem((6,))],
+        scratch_shapes=[pltpu.VMEM(one.shape, one.dtype) for one in (shapes[0], codes, shapes[2])] + [pltpu.VMEM((n_sp * size, chan), F32), sem((6,))],
     )(*held)
     return (result[None, None], wgrad.reshape(weights.shape), grad_in[None, None])
 

time: 33.6 us -> 33.3 us (level)
  no operation moved by 1% of the time
where the time goes in v5:
time: 33.3 us; the launch traced here: 33.1 us
  Pallas kernels  32.5 us (98%)
  between operations  0.64 us (2%)
    pallas_call x1, Pallas kernels, per_device(): pl.pallas_call(functools.partial(block_kernel, n_sp, n_dp, side), out_sha...  30 us
    pallas_call x1, Pallas kernels, per_device(): pl.pallas_call(hand_on, out_shape=shapes, in_specs=[hbm, hbm, hbm], out_s...  2.5 us

profile of v5, /device:TPU:0, one launch (start us, length us, event | category | flops | bytes accessed | tf_op | source)
XLA Modules:
  0.0 33.1 jit_solution(13706349151482958290)
XLA Ops:
  0.6 30.0 %shard_map.76 = (bf16[56,56,128]{2,1,0:T(8,128)(2,1)}, s16[8,160,128]{2,1,0:T(8,128)(2,1)}, bf16[56,56,128]{2,1,0:T(8,128)(2,1)}) custom-call(s32[1,2,8]{2,1,0:T(2,128)} %bitcast.11, bf16[56,56,128]{2,1,0:T(8,128)(2,1)} %bitcast.8, bf16[3,384,128]{2,1,0:T(8,128)(2,1)} %bitcast.10, f32[1,128]{1,0:T(1,128)} %bitcast.12, bf16[56,56,128]{2,1,0:T(8,128)(2,1)} %bitcast.9), custom_call_target="tpu_custom_call" | custom-call | tf_op jit(solution)/shard_map/pallas_call | solution.py:431
  30.6 2.5 %shard_map.77 = (bf16[56,56,128]{2,1,0:T(8,128)(2,1)}, f32[1152,128]{1,0:T(8,128)}, bf16[56,56,128]{2,1,0:T(8,128)(2,1)}) custom-call(bf16[56,56,128]{2,1,0:T(8,128)(2,1)} %get-tuple-element.9.a_in, s16[8,160,128]{2,1,0:T(8,128)(2,1)} %get-tuple-element.10.codes_in, bf16[56,56,128]{2,1,0:T(8,128)(2,1)} %get-tuple-element.11.c_in), custom_call_target="tpu_custom_call" | custom-call | tf_op jit(solution)/shard_map/pallas_call | solution.py:464
